TPU v7x, 256 devices: a whole 4x4x8 slice. The times are simulated.
256 devices in a mesh: ctx: 16 (over z, core), exp: 16 (over x, y).
Axes of the slice: x: 4, y: 4, z: 8, core: 2. Of those that a mesh axis runs over, the one named last changes fastest.
Arguments:
- inner_input: bfloat16 [8192, 8192], P('ctx', 'exp'), may hold values from -6 to 6
- gate_input: bfloat16 [8192, 8192], P('ctx', 'exp'), may hold values from -6 to 6
- coupling_input: bfloat16 [8192, 256], P('ctx'), may hold values from -6 to 6
- step_input: float32 [8192, 128], P('ctx', 'exp'), may hold values from -7 to 140
- conv_inner: float32 [4, 8192], P(None, 'exp'), may hold values from -3 to 3
- conv_coupling: float32 [4, 256], replicated, may hold values from -3 to 3
- decay_log: float32 [128], P('exp'), may hold values from -5.3 to -2.5
- skip_gain: float32 [128], P('exp'), may hold values from 0.5 to 2
- norm_gain: float32 [8192], P('exp'), may hold values from 0.1 to 1.9
- out_weight: bfloat16 [8192, 4096], P('exp'), may hold values from -0.0625 to 0.0625
- residual: bfloat16 [8192, 4096], P(('ctx', 'exp')), may hold values from -6 to 6
- moe_gain: float32 [4096], replicated, may hold values from 0.1 to 1.9
- router_weight: bfloat16 [4096, 72], replicated, may hold values from -0.1875 to 0.1875
- routes: int32 [8192, 10], P(('ctx', 'exp')), may hold values from 0 to 71, all different within a row
- priority: int32 [256, 32], P(('ctx', 'exp')), may hold values from 0 to 31, each once within a row
- expert_in: bfloat16 [16, 4096, 1536], P('exp', 'ctx'), may hold values from -0.09375 to 0.09375
- expert_out: bfloat16 [16, 4096, 768], P('exp', 'ctx'), may hold values from -0.21875 to 0.21875
Outputs:
- hidden: float32 [8192, 4096], P(('ctx', 'exp'))
- moe_out: float32 [8192, 4096], P(('ctx', 'exp'))
Inputs may be any that keep to these rules, and one draw needn't show every extreme that they name: `routes`: each token names 10 different experts. `priority`: the 32 tokens of each row carry distinct priorities.
All inputs are finite; a program needn't handle non-finite values.
Results may differ from a plain program's by a relative error of at most 0.029.
Values may be sent and summed in bfloat16 or wider, within the bound.
A program may use at most 128 MiB of HBM per device.

v0:
```python
import jax
import jax.numpy as jnp
from jax import lax
from jax.sharding import PartitionSpec as P

HDIM = 64
STATE = 128
KCONV = 4
NEXP = 72
TOPK = 10
FFE = 768
SPAN = 256
INNER = 8192
EPS = 1e-05
HIGH = lax.Precision.HIGHEST


def shifted(array, axis, by):
    devices = lax.axis_size(axis)
    pairs = [(i, i + by) for i in range(devices) if 0 <= i + by < devices]
    return lax.ppermute(array, axis, pairs)


def carried_in(part, axis, combine, identity):
    place = lax.axis_index(axis)
    gathered = jax.tree.map(lambda a: lax.all_gather(a, axis), part)
    state = jax.tree.map(lambda a, e: jnp.zeros_like(a) + jnp.asarray(e, a.dtype), part, identity)

    def one(step, state):
        return combine(
            state, jax.tree.map(lambda a: lax.dynamic_index_in_dim(a, step, 0, False), gathered)
        )

    return lax.fori_loop(0, place, one, state)


def causal_conv(values, before, weight):
    count = values.shape[0]
    padded = jnp.concatenate([before.astype(jnp.float32), values.astype(jnp.float32)], axis=0)
    total = jnp.zeros((count, values.shape[1]), jnp.float32)
    for k in range(KCONV):
        total = total + weight[k][None, :] * padded[k : k + count]
    return jax.nn.silu(total).astype(jnp.bfloat16)


def join_states(earlier, later):
    return (earlier[0] * later[0], later[0][:, None, None] * earlier[1] + later[1])


def body(
    inner_input,
    gate_input,
    coupling_input,
    step_input,
    conv_inner,
    conv_coupling,
    decay_log,
    skip_gain,
    norm_gain,
    out_weight,
    residual,
    moe_gain,
    router_weight,
    routes,
    priority,
    expert_in,
    expert_out,
):
    width = inner_input.shape[1]
    heads = decay_log.shape[0]
    count = inner_input.shape[0]
    blocks = count // SPAN
    edges = jnp.concatenate(
        [inner_input[count - (KCONV - 1) :], coupling_input[count - (KCONV - 1) :]], axis=1
    )
    before = shifted(edges, "ctx", 1)
    inner = causal_conv(inner_input, before[:, :width], conv_inner)
    coupling = causal_conv(coupling_input, before[:, width:], conv_coupling)
    steps = jax.nn.softplus(step_input).reshape(blocks, SPAN, heads)
    inner_parts = inner.reshape(blocks, SPAN, heads, HDIM)
    input_parts = coupling[:, :STATE].reshape(blocks, SPAN, STATE)
    output_parts = coupling[:, STATE:].reshape(blocks, SPAN, STATE)
    rate = steps * (-jnp.exp(decay_log))[None, None, :]
    cums = jnp.cumsum(rate, axis=1)
    scores = jnp.einsum(
        "cin,cjn->cij", output_parts, input_parts, preferred_element_type=jnp.float32
    )
    above = (jnp.arange(SPAN)[:, None] >= jnp.arange(SPAN)[None, :])[None, None]
    flipped = jnp.swapaxes(cums, 1, 2)
    spread = flipped[:, :, :, None] - flipped[:, :, None, :]
    decay = jnp.where(above, jnp.exp(jnp.where(above, spread, 0.0)), 0.0)
    mixing = (scores[:, None] * decay * jnp.swapaxes(steps, 1, 2)[:, :, None, :]).astype(
        jnp.bfloat16
    )
    local = jnp.einsum("chij,cjhp->cihp", mixing, inner_parts, preferred_element_type=jnp.float32)
    inner_wide = inner_parts.astype(jnp.float32)
    tail = jnp.exp(cums[:, -1:, :] - cums) * steps
    states = jnp.einsum(
        "cjh,cjn,cjhp->chnp", tail, input_parts.astype(jnp.float32), inner_wide, precision=HIGH
    )
    drops = jnp.exp(cums[:, -1, :])
    running = jnp.zeros((heads, STATE, HDIM), jnp.float32)
    reach = jnp.ones((heads,), jnp.float32)
    starts = []
    reaches = []
    for k in range(blocks):
        starts.append(running)
        reaches.append(reach)
        running = drops[k][:, None, None] * running + states[k]
        reach = reach * drops[k]
    neutral = (jnp.ones((heads,), jnp.float32), jnp.zeros((heads, STATE, HDIM), jnp.float32))
    incoming = carried_in((reach, running), "ctx", join_states, neutral)[1]
    entry = jnp.stack([reaches[k][:, None, None] * incoming + starts[k] for k in range(blocks)])
    carried = jnp.einsum(
        "cin,cih,chnp->cihp", output_parts.astype(jnp.float32), jnp.exp(cums), entry, precision=HIGH
    )
    mixed = (local + carried + skip_gain[None, None, :, None] * inner_wide).reshape(count, width)
    gated = mixed * jax.nn.silu(gate_input.astype(jnp.float32))
    squares = jnp.sum(gated * gated, axis=1)
    scaled = (gated * norm_gain[None, :]).astype(jnp.bfloat16)
    projected = jnp.dot(scaled, out_weight, preferred_element_type=jnp.float32)
    owned = lax.psum_scatter(
        projected.astype(jnp.bfloat16), "exp", scatter_dimension=0, tiled=True
    ).astype(jnp.float32)
    owned_squares = lax.psum_scatter(squares, "exp", scatter_dimension=0, tiled=True)
    mamba_out = owned * lax.rsqrt(owned_squares / INNER + EPS)[:, None]
    hidden = residual.astype(jnp.float32) + mamba_out
    tokens = hidden.shape[0]
    flight = lax.axis_size("exp")
    capacity = max(2, 2 * tokens * TOPK // NEXP)
    normed = (
        hidden * lax.rsqrt(jnp.mean(hidden * hidden, axis=1) + EPS)[:, None] * moe_gain[None, :]
    ).astype(jnp.bfloat16)
    logits = jnp.dot(normed, router_weight, preferred_element_type=jnp.float32)
    table = routes[:, :, None] == jnp.arange(NEXP, dtype=jnp.int32)[None, None, :]
    picked = jnp.sum(jnp.where(table, logits[:, None, :], 0.0), axis=2)
    raised = jnp.exp(picked)
    probs = raised / jnp.sum(raised, axis=1, keepdims=True)
    match = routes[:, :, None] == jnp.arange(flight, dtype=jnp.int32)[None, None, :]
    member = jnp.sum(match.astype(jnp.int32), axis=1)
    share = jnp.sum(jnp.where(match, probs[:, :, None], 0.0), axis=1).astype(jnp.bfloat16)
    order = priority[0]
    earlier = (order[None, :] < order[:, None]).astype(jnp.int32)
    rank = jnp.sum(earlier[:, :, None] * member[None, :, :], axis=1)
    kept = (member > 0) & (rank < capacity)
    slots = kept[:, :, None] & (
        rank[:, :, None] == jnp.arange(capacity, dtype=jnp.int32)[None, None, :]
    )
    select = jnp.transpose(slots, (1, 2, 0)).astype(jnp.bfloat16)
    outbound = jnp.einsum("fst,td->fsd", select, normed, preferred_element_type=jnp.float32).astype(
        jnp.bfloat16
    )
    arrived = lax.all_to_all(outbound, "exp", split_axis=0, concat_axis=0, tiled=True)
    rows = arrived.reshape(flight * capacity, normed.shape[1])
    slices = lax.axis_size("ctx")
    whole_in = lax.all_gather(expert_in[0], "ctx", axis=0, tiled=True)
    slice_width = rows.shape[1] // slices
    parts = jnp.einsum(
        "rkw,kwf->krf",
        rows.reshape(rows.shape[0], slices, slice_width),
        whole_in.reshape(slices, slice_width, 2 * FFE),
        preferred_element_type=jnp.float32,
    ).astype(jnp.bfloat16)
    units = jnp.sum(lax.optimization_barrier(parts).astype(jnp.float32), axis=0)
    activated = (jax.nn.silu(units[:, :FFE]) * units[:, FFE:]).astype(jnp.bfloat16)
    answer = jnp.einsum(
        "rf,df->rd",
        activated,
        lax.all_gather(expert_out[0], "ctx", axis=0, tiled=True),
        preferred_element_type=jnp.float32,
    ).astype(jnp.bfloat16)
    returned = lax.all_to_all(
        answer.reshape(flight, capacity, answer.shape[1]),
        "exp",
        split_axis=0,
        concat_axis=0,
        tiled=True,
    )
    weights = select * jnp.transpose(share)[:, None, :]
    moe_out = jnp.einsum("fst,fsd->td", weights, returned, preferred_element_type=jnp.float32)
    return (hidden, moe_out)


def solution(mesh):
    placed = (
        P("ctx", "exp"),
        P("ctx", "exp"),
        P("ctx", None),
        P("ctx", "exp"),
        P(None, "exp"),
        P(),
        P("exp"),
        P("exp"),
        P("exp"),
        P("exp", None),
        P(("ctx", "exp"), None),
        P(),
        P(),
        P(("ctx", "exp"), None),
        P(("ctx", "exp"), None),
        P("exp", "ctx", None),
        P("exp", "ctx", None),
    )
    return jax.shard_map(
        body,
        mesh=mesh,
        in_specs=placed,
        out_specs=(P(("ctx", "exp"), None), P(("ctx", "exp"), None)),
        check_vma=False,
    )
```

profile of v0, /device:TPU:32, one launch (start us, length us, event | category | flops | bytes accessed | tf_op | source)
XLA Modules:
  0.0 354.1 jit_solution(14720117451480724429)
XLA Ops:
  7.2 0.8 slice.91
  8.0 0.7 slice.92
  8.7 0.8 copy.91
  9.5 1.9 collective-permute-start
  11.4 0.7 compare_select_fusion
  12.2 0.7 exponential_negate_fusion
  12.9 1.1 reduce-window.6
  14.3 0.7 fusion.63
  15.2 0.8 fusion.66
  16.0 0.9 fusion.65
  16.9 0.6 slice_bitcast_fusion.1
  17.5 1.0 convert_element_type.80
  18.5 1.3 copy.92
  20.4 1.5 multiply_convert_fusion.9
  22.0 0.7 convolution_bitcast_fusion.1
  22.7 0.8 slice_add_fusion
  23.8 19.0 %all-gather.2 = f32[16,1,8]{2,1,0:T(1,128)} all-gather(f32[1,1,8]{2,1,0:T(1,128)S(1)} %get-tuple-element.98), channel_id=1, replica_groups=mesh['ctx'=16,'exp'=16] {'ctx'}, dimensions={0}, use_global_device_ids=true | all-gather | bytes 544 | tf_op jit(solution)/shard_map/all_gather | solution.py:26
  42.9 0.7 add_bitcast_fusion.1
  43.5 1.0 fusion.67
  44.6 24.1 %all-gather.7.cloned.1.call-done = f32[16,8,128,64]{2,3,1,0:T(8,128)} async-done(((f32[1,8,128,64]{2,3,1,0:T(8,128)}), f32[16,8,128,64]{2,3,1,0:T(8,128)}) %all-gather.7.cloned.1.call-update) | async-done | bytes 4194320 | tf_op jit(solution)/shard_map/all_gather | solution.py:26
  68.7 4.1 %while.12 = (s32[]{:T(128)}, f32[8,128,64]{2,1,0:T(8,128)S(1)}, s32[]{:T(128)}, f32[16,8]{1,0:T(8,128)}, f32[16,8,128,64]{2,3,1,0:T(8,128)}, /*index=5*/s32[]{:T(128)}, s32[]{:T(128)}, s32[]{:T(128)}) while((s32[]{:T(128)}, f32[8,128,64]{2,1,0:T(8,128)S(1)}, s32[]{:T(128)}, f32[16,8]{1,0:T(8,128)}, f32[16,8,128,64]{2,3,1,0:T(8,128)}, ...), condition=%wide.region_3.4_spmd, body=%wide.region_2.3_spmd.sunk | while | flops 131077 | bytes 1835231 | solution.py:34
  68.8 1.0 constant_dynamic-slice_fusion.2
  69.9 0.7 dynamic-slice_bitcast_fusion.2
  70.8 1.0 constant_dynamic-slice_fusion.2
  72.0 0.7 dynamic-slice_bitcast_fusion.2
  73.0 0.8 fusion.47
  73.9 1.5 fusion.68
  75.4 2.3 fusion.17
  77.7 0.8 copy.101
  78.6 1.3 copy-done.10
  79.9 4.6 %convolution_convert_fusion = bf16[512,4096]{1,0:T(8,128)(2,1)} fusion(bf16[512,4096]{1,0:T(8,128)(2,1)S(1)} %copy-done.10, f32[512]{0:T(512)S(1)} %copy-done.11, f32[512,512]{0,1:T(8,128)S(1)} %bitcast.109, bf16[512,512]{0,1:T(8,128)(2,1)S(1)} %copy.102), kind=kOutput, calls=%fused_computation.6 | convolution fusion | flops 2151677952 | bytes 9963520 | tf_op jit(solution)/shard_map/dot_general | solution.py:121
  84.6 0.7 all-gather.9.cloned.1.call-update
  85.4 0.5 all-gather.11.cloned.1.call-update
  86.0 0.6 multiply_reduce_fusion.2
  86.7 0.6 dynamic-slice
  88.4 40.4 %all-reduce = f32[512]{0:T(512)S(1)} all-reduce(f32[512]{0:T(512)S(1)} %multiply_reduce_fusion), channel_id=5, replica_groups=mesh['ctx'=16,'exp'=16] {'exp'}, use_global_device_ids=true, to_apply=%region_6.7.clone | all-reduce | flops 512 | bytes 4096
  128.9 63.8 %reduce-scatter.2.cloned.1.call-done = bf16[32,4096]{1,0:T(8,128)(2,1)} async-done(((bf16[512,4096]{1,0:T(8,128)(2,1)}), bf16[32,4096]{1,0:T(8,128)(2,1)}) %reduce-scatter.2.cloned.1.call-update) | async-done | bytes 262160 | tf_op jit(solution)/shard_map/reduce_scatter | solution.py:122
  192.6 1.2 multiply_reduce_fusion.1
  193.9 0.5 convolution_convert_fusion.2
  194.4 19.8 %all_to_all.10 = bf16[16,8,4096]{2,1,0:T(8,128)(2,1)S(1)} all-to-all(bf16[16,8,4096]{2,1,0:T(8,128)(2,1)S(1)} %convolution_convert_fusion.2), channel_id=1, replica_groups=mesh['ctx'=16,'exp'=16] {'exp'}, dimensions={0} | all-to-all | bytes 2097152 | tf_op jit(solution)/shard_map/all_to_all | solution.py:153
  214.5 53.0 %all-gather.9.cloned.1.call-done = bf16[1,4096,1536]{2,1,0:T(8,128)(2,1)} async-done(((bf16[1,256,1536]{2,1,0:T(8,128)(2,1)}), bf16[1,4096,1536]{2,1,0:T(8,128)(2,1)}) %all-gather.9.cloned.1.call-update) | async-done | bytes 12582928 | tf_op jit(solution)/shard_map/all_gather | solution.py:156
  267.5 6.6 %convolution_convert_fusion.1 = bf16[16,128,1536]{2,1,0:T(8,128)(2,1)S(1)} fusion(bf16[16,256,1536]{2,1,0:T(8,128)(2,1)} %bitcast.107, bf16[128,16,256]{2,1,0:T(8,128)(2,1)S(1)} %bitcast.108), kind=kOutput, calls=%fused_computation.7 | convolution fusion | flops 1613758464 | bytes 19922944 | tf_op jit(solution)/shard_map/rkw,kwf->krf/dot_general | solution.py:158
  274.1 0.9 convert_reduce_fusion
  275.0 40.1 %all-gather.11.cloned.1.call-done = bf16[1,4096,768]{2,1,0:T(8,128)(2,1)} async-done(((bf16[1,256,768]{2,1,0:T(8,128)(2,1)}), bf16[1,4096,768]{2,1,0:T(8,128)(2,1)}) %all-gather.11.cloned.1.call-update) | async-done | bytes 6291472 | tf_op jit(solution)/shard_map/all_gather | solution.py:169
  315.1 5.9 %fusion.5 = bf16[16,8,4096]{2,1,0:T(8,128)(2,1)} fusion(bf16[1,4096,768]{2,1,0:T(8,128)(2,1)} %all-gather.11.cloned.1.call-done, f32[128,1536]{1,0:T(8,128)S(1)} %convert_reduce_fusion), kind=kOutput, calls=%fused_computation.10 | convolution fusion | flops 806420480 | bytes 8126464 | tf_op jit(solution)/shard_map/rf,df->rd/dot_general | solution.py:166
  321.0 6.8 %all-to-all-start.1 = ((bf16[16,8,4096]{2,1,0:T(8,128)(2,1)}), bf16[16,8,4096]{2,1,0:T(8,128)(2,1)S(1)}, u32[]{:S(2)}, u32[]{:S(2)}) async-start(bf16[16,8,4096]{2,1,0:T(8,128)(2,1)} %fusion.5), calls=%async_computation.2 | async-start | bytes 2097152 | tf_op jit(solution)/shard_map/all_to_all | solution.py:172
  328.4 17.6 %all-to-all-done.1 = bf16[16,8,4096]{2,1,0:T(8,128)(2,1)S(1)} async-done(((bf16[16,8,4096]{2,1,0:T(8,128)(2,1)}), bf16[16,8,4096]{2,1,0:T(8,128)(2,1)S(1)}, u32[]{:S(2)}, u32[]{:S(2)}) %all-to-all-start.1) | async-done | bytes 1048608 | tf_op jit(solution)/shard_map/all_to_all | solution.py:172
  346.0 1.5 convolution_bitcast_fusion
  (73 shorter events, 4.3 us)
Async XLA Ops:
  7.2 320.6 %copy-start = (bf16[4096,72]{0,1:T(8,128)(2,1)S(1)}, bf16[4096,72]{0,1:T(8,128)(2,1)}, u32[]{:S(2)}) copy-start(bf16[4096,72]{0,1:T(8,128)(2,1)} %param.31) | copy-start | bytes 1769476
  7.2 61.5 %all-gather.7.cloned.1.call-start = ((), (), s32[]{:S(2)}) async-start(), calls=%async_computation.3 | async-start | bytes 4456448 | tf_op jit(solution)/shard_map/all_gather | solution.py:26
  9.5 10.3 %collective-permute-start = (bf16[3,768]{0,1:T(8,128)(2,1)}, bf16[3,768]{0,1:T(8,128)(2,1)S(1)}, u32[]{:S(2)}, u32[]{:S(2)}) collective-permute-start(bf16[3,768]{0,1:T(8,128)(2,1)} %copy.91), channel_id=1, source_target_pairs={{0,16},{16,32},{32,48},{48,64},{64,80},{80,96},{96,112},{112,128},... | collective-permute-start | bytes 13832 | tf_op jit(solution)/shard_map/ppermute | solution.py:21
  17.5 5.2 %copy-start.8 = (f32[8]{0:T(128)}, f32[8]{0:T(128)S(1)}, u32[]{:S(2)}) copy-start(f32[8]{0:T(128)S(1)} %broadcast_multiply_fusion) | copy-start | bytes 100
  19.7 3.9 %copy-start.4 = (bf16[512,512]{1,0:T(8,128)(2,1)S(1)}, bf16[512,512]{1,0:T(8,128)(2,1)}, u32[]{:S(2)}) copy-start(bf16[512,512]{1,0:T(8,128)(2,1)} %param.20) | copy-start | bytes 1572868
  20.4 48.3 %copy-start.2 = (bf16[512,128]{1,0:T(8,128)(2,1)}, bf16[512,128]{1,0:T(8,128)(2,1)S(1)}, u32[]{:S(2)}) copy-start(bf16[512,128]{1,0:T(8,128)(2,1)S(1)} %get-tuple-element.87) | copy-start | bytes 393220
  23.5 169.1 %reduce-scatter.2.cloned.1.call-start = ((), (), s32[]{:S(2)}) async-start(), calls=%async_computation.4 | async-start | bytes 4456448 | tf_op jit(solution)/shard_map/reduce_scatter | solution.py:122
  72.8 2.5 copy-start.3
  77.7 2.2 copy-start.10
  77.7 2.2 copy-start.11
  84.5 1.4 copy-start.6
  84.5 1.4 copy-start.9
  84.5 2.2 copy-start.12
  84.5 108.1 %copy-start.5 = (bf16[32,4096]{1,0:T(8,128)(2,1)S(1)}, bf16[32,4096]{1,0:T(8,128)(2,1)}, u32[]{:S(2)}) copy-start(bf16[32,4096]{1,0:T(8,128)(2,1)} %param.29) | copy-start | bytes 786436
  84.6 109.3 %copy-start.7 = (f32[4096]{0:T(1024)S(1)}, f32[4096]{0:T(1024)}, u32[]{:S(2)}) copy-start(f32[4096]{0:T(1024)} %param.30) | copy-start | bytes 49156
  84.6 182.9 %all-gather.9.cloned.1.call-start = ((), (), s32[]{:S(2)}) async-start(), calls=%async_computation.5 | async-start | bytes 13369344 | tf_op jit(solution)/shard_map/all_gather | solution.py:156
  85.3 229.7 %all-gather.11.cloned.1.call-start = ((), (), s32[]{:S(2)}) async-start(), calls=%async_computation.6 | async-start | bytes 6684672 | tf_op jit(solution)/shard_map/all_gather | solution.py:169
  193.9 133.9 %copy-start.1 = (f32[32,4096]{1,0:T(8,128)}, f32[32,4096]{1,0:T(8,128)S(1)}, u32[]{:S(2)}) copy-start(f32[32,4096]{1,0:T(8,128)S(1)} %get-tuple-element.83) | copy-start | bytes 1572868
  321.0 25.0 %all-to-all-start.1 = ((bf16[16,8,4096]{2,1,0:T(8,128)(2,1)}), bf16[16,8,4096]{2,1,0:T(8,128)(2,1)S(1)}, u32[]{:S(2)}, u32[]{:S(2)}) async-start(bf16[16,8,4096]{2,1,0:T(8,128)(2,1)} %fusion.5), calls=%async_computation.2 | async-start | bytes 2097152 | tf_op jit(solution)/shard_map/all_to_all | solution.py:172
Sparse Core Ops, SparseCore 0:
  23.6 44.9 all-gather.6
  84.7 107.8 reduce-scatter.1
  194.5 72.9 all-gather.8
  269.2 45.8 all-gather.10
where the time goes:
time: 356 us; the launch traced here: 354 us
  waiting for transfers between devices  200 us (56%)
  blocking collectives  79.3 us (22%)
  matrix products  25.1 us (7%)
  between operations  14.8 us (4%)
  local copies, waits for them, and re-layouts  13.1 us (4%)
  other arithmetic  13.1 us (4%)
  starting transfers between devices  8.84 us (2%)
    reduce_scatter x1, waiting for transfers between devices, body(): lax.psum_scatter(projected.astype(jnp.bfloat16), 'exp', scatter_dimension...  63.8 us
    all_gather x1, waiting for transfers between devices, body(): whole_in = lax.all_gather(expert_in[0], 'ctx', axis=0, tiled=True)  53 us
    unnamed x1, blocking collectives  40.4 us
    all_gather x1, waiting for transfers between devices, body(): lax.all_gather(expert_out[0], 'ctx', axis=0, tiled=True)  40.1 us
    all_gather x1, waiting for transfers between devices, carried_in(): gathered = jax.tree.map(lambda a: lax.all_gather(a, axis), part)  24.1 us
    all_to_all x1, blocking collectives, body(): lax.all_to_all(outbound, 'exp', split_axis=0, concat_axis=0, tiled=True)  19.8 us
    all_gather x1, blocking collectives, carried_in(): gathered = jax.tree.map(lambda a: lax.all_gather(a, axis), part)  19 us
    all_to_all x1, waiting for transfers between devices, body(): lax.all_to_all(answer.reshape(flight, capacity, answer.shape[1]), 'exp',...  17.6 us
  transfers between devices with their start and end apart: 6, of which 5 were waited for; matrix products, arithmetic and copies ran while one was open for 6% of the time, Pallas kernels for 0%

commit v1 on v0

--- a/solution.py
+++ b/solution.py
@@ -13,6 +13,20 @@
 INNER = 8192
 EPS = 1e-05
 HIGH = lax.Precision.HIGHEST
+
+
+def on_each_block(array, axis, dim, make, out_dim):
+    ways, here, step = (lax.axis_size(axis), lax.axis_index(axis), array.shape[dim])
+    earlier, later = ([], [])
+    going_up = going_down = array
+    for far in range(ways // 2 + 1):
+        earlier.append(make(going_up, (here - far) % ways * step))
+        if 0 < far < ways - ways // 2:
+            later.append(make(going_down, (here + far) % ways * step))
+        going_up = lax.ppermute(going_up, axis, [(d, (d + 1) % ways) for d in range(ways)])
+        going_down = lax.ppermute(going_down, axis, [(d, (d - 1) % ways) for d in range(ways)])
+    line = jnp.concatenate([*earlier[::-1], *later], axis=out_dim)
+    return jnp.roll(line, (here - ways // 2) * earlier[0].shape[out_dim], axis=out_dim)
 
 
 def shifted(array, axis, by):
@@ -163,11 +177,14 @@
     ).astype(jnp.bfloat16)
     units = jnp.sum(lax.optimization_barrier(parts).astype(jnp.float32), axis=0)
     activated = (jax.nn.silu(units[:, :FFE]) * units[:, FFE:]).astype(jnp.bfloat16)
-    answer = jnp.einsum(
-        "rf,df->rd",
-        activated,
-        lax.all_gather(expert_out[0], "ctx", axis=0, tiled=True),
-        preferred_element_type=jnp.float32,
+    answer = on_each_block(
+        expert_out[0],
+        "ctx",
+        0,
+        lambda shard, offset: jnp.einsum(
+            "rf,df->rd", activated, shard, preferred_element_type=jnp.float32
+        ),
+        1,
     ).astype(jnp.bfloat16)
     returned = lax.all_to_all(
         answer.reshape(flight, capacity, answer.shape[1]),

time: 356 us -> 325 us (0.913)
  waiting for transfers between devices: 200 us -> 150 us
  starting transfers between devices: 8.84 us -> 38.9 us
  blocking collectives: 79.3 us -> 58.5 us
  matrix products: 25.1 us -> 32.1 us
    reduce_scatter x1, waiting for transfers between devices: 63.8 us -> 15 us  [body(): lax.psum_scatter(projected.astype(jnp.bfloat16), 'exp', scatter_dimension...]
    ppermute x0 -> x15, waiting for transfers between devices: none -> 42.6 us  [the longest x8 21.9 us: on_each_block(): lax.ppermute(going_up, axis, [(d, (d + 1) % ways) for d in range(ways)])]
    all_gather x1 -> x0, waiting for transfers between devices: 40.1 us -> none  [body(): lax.all_gather(expert_out[0], 'ctx', axis=0, tiled=True)]
    ppermute x0 -> x15, starting transfers between devices: none -> 24.9 us  [the longest x7 21.1 us: on_each_block(): lax.ppermute(going_down, axis, [(d, (d - 1) % ways) for d in range(ways)])]
    all_to_all x1 -> x0, blocking collectives: 19.8 us -> none  [body(): lax.all_to_all(outbound, 'exp', split_axis=0, concat_axis=0, tiled=True)]
    dot_general x1 -> x16, matrix products: 5.92 us -> 13.8 us  [body(): jnp.einsum('rf,df->rd', activated, shard, preferred_element_type=jnp.floa...]
    all_to_all x0 -> x1, starting transfers between devices: none -> 4.8 us  [body(): lax.all_to_all(outbound, 'exp', split_axis=0, concat_axis=0, tiled=True)]
    all_gather x1, waiting for transfers between devices: 53 us -> 49.1 us  [body(): whole_in = lax.all_gather(expert_in[0], 'ctx', axis=0, tiled=True)]
  transfers between devices with their start and end apart: 6 -> 21, of which waited for: 5 -> 13; matrix products, arithmetic and copies ran while one was open for 6% -> 11% of each run, Pallas kernels for 0% -> 0%
where the time goes in v1:
time: 325 us; the launch traced here: 323 us
  waiting for transfers between devices  150 us (46%)
  blocking collectives  58.5 us (18%)
  starting transfers between devices  38.9 us (12%)
  matrix products  32.1 us (10%)
  between operations  15.2 us (5%)
  other arithmetic  14.1 us (4%)
  local copies, waits for them, and re-layouts  13.6 us (4%)
    all_gather x1, waiting for transfers between devices, body(): whole_in = lax.all_gather(expert_in[0], 'ctx', axis=0, tiled=True)  49.1 us
    unnamed x1, blocking collectives  40.6 us
    all_gather x1, waiting for transfers between devices, carried_in(): gathered = jax.tree.map(lambda a: lax.all_gather(a, axis), part)  25.3 us
    ppermute x8, waiting for transfers between devices, on_each_block(): lax.ppermute(going_up, axis, [(d, (d + 1) % ways) for d in range(ways)])  21.9 us
    ppermute x7, starting transfers between devices, on_each_block(): lax.ppermute(going_down, axis, [(d, (d - 1) % ways) for d in range(ways)])  21.1 us
    ppermute x7, waiting for transfers between devices, on_each_block(): lax.ppermute(going_down, axis, [(d, (d - 1) % ways) for d in range(ways)])  20.7 us
    all_gather x1, blocking collectives, carried_in(): gathered = jax.tree.map(lambda a: lax.all_gather(a, axis), part)  17.9 us
    all_to_all x1, waiting for transfers between devices, body(): lax.all_to_all(answer.reshape(flight, capacity, answer.shape[1]), 'exp',...  17.6 us
  transfers between devices with their start and end apart: 21, of which 13 were waited for; matrix products, arithmetic and copies ran while one was open for 11% of the time, Pallas kernels for 0%

profile of v1, /device:TPU:32, one launch (start us, length us, event | category | flops | bytes accessed | tf_op | source)
XLA Modules:
  0.0 322.8 jit_solution(17004461405221099722)
XLA Ops:
  8.9 1.9 collective-permute-start
  12.3 1.1 reduce-window.6
  14.8 1.4 fusion.57
  17.4 1.0 convert_element_type.80
  18.4 1.3 copy.92
  20.3 2.2 multiply_convert_fusion.9
  23.4 1.5 slice_add_fusion
  25.3 17.9 %all-gather.1 = f32[16,1,8]{2,1,0:T(1,128)S(1)} all-gather(f32[1,1,8]{2,1,0:T(1,128)S(1)} %copy-done.28), channel_id=1, replica_groups=mesh['ctx'=16,'exp'=16] {'ctx'}, dimensions={0}, use_global_device_ids=true | all-gather | bytes 544 | tf_op jit(solution)/shard_map/all_gather | solution.py:40
  43.8 1.0 fusion.59
  44.9 25.3 %all-gather.5.cloned.1.call-done = f32[16,8,128,64]{2,3,1,0:T(8,128)} async-done(((f32[1,8,128,64]{2,3,1,0:T(8,128)}), f32[16,8,128,64]{2,3,1,0:T(8,128)}) %all-gather.5.cloned.1.call-update) | async-done | bytes 4194320 | tf_op jit(solution)/shard_map/all_gather | solution.py:40
  70.2 2.8 while.12
  74.5 1.5 fusion.9
  76.9 1.3 copy-done.29
  78.2 4.5 %convolution_convert_fusion = bf16[512,4096]{1,0:T(8,128)(2,1)} fusion(bf16[512,4096]{1,0:T(8,128)(2,1)S(1)} %copy-done.29, f32[512]{0:T(512)S(1)} %copy-done.30, f32[512,512]{0,1:T(8,128)S(1)} %bitcast.138, bf16[512,512]{0,1:T(8,128)(2,1)S(1)} %copy.102), kind=kOutput, calls=%fused_computation.4 | convolution fusion | flops 2151677952 | bytes 9963520 | tf_op jit(solution)/shard_map/dot_general | solution.py:135
  83.7 1.6 collective-permute-start.1
  85.5 5.5 %collective-permute-done.1 = bf16[256,768]{1,0:T(8,128)(2,1)S(1)} collective-permute-done((bf16[256,768]{1,0:T(8,128)(2,1)S(1)}, bf16[256,768]{1,0:T(8,128)(2,1)S(1)}, u32[]{:S(2)}, u32[]{:S(2)}) %collective-permute-start.1) | collective-permute-done | bytes 393248 | tf_op jit(solution)/shard_map/ppermute | solution.py:26
  92.7 5.4 %collective-permute-done.2 = bf16[256,768]{1,0:T(8,128)(2,1)S(1)} collective-permute-done((bf16[256,768]{1,0:T(8,128)(2,1)S(1)}, bf16[256,768]{1,0:T(8,128)(2,1)S(1)}, u32[]{:S(2)}, u32[]{:S(2)}) %collective-permute-start.2) | collective-permute-done | bytes 393248 | tf_op jit(solution)/shard_map/ppermute | solution.py:26
  101.1 12.1 %collective-permute-start.11 = (bf16[256,768]{1,0:T(8,128)(2,1)S(1)}, bf16[256,768]{1,0:T(8,128)(2,1)}, u32[]{:S(2)}, u32[]{:S(2)}) collective-permute-start(bf16[256,768]{1,0:T(8,128)(2,1)S(1)} %collective-permute-done.10), channel_id=1, source_target_pairs={{0,240},{16,0},{32,16},{48,32},{64,48},{80,64},{96,80},{112,96},{1... | collective-permute-start | bytes 1179656 | tf_op jit(solution)/shard_map/ppermute | solution.py:27
  113.2 3.5 %collective-permute-done.3 = bf16[256,768]{1,0:T(8,128)(2,1)} collective-permute-done((bf16[256,768]{1,0:T(8,128)(2,1)S(1)}, bf16[256,768]{1,0:T(8,128)(2,1)}, u32[]{:S(2)}, u32[]{:S(2)}) %collective-permute-start.3) | collective-permute-done | bytes 393248 | tf_op jit(solution)/shard_map/ppermute | solution.py:26
  116.7 1.8 collective-permute-done.11
  118.5 3.4 %collective-permute-start.12 = (bf16[256,768]{1,0:T(8,128)(2,1)}, bf16[256,768]{1,0:T(8,128)(2,1)}, u32[]{:S(2)}, u32[]{:S(2)}) collective-permute-start(bf16[256,768]{1,0:T(8,128)(2,1)} %collective-permute-done.11), channel_id=1, source_target_pairs={{0,240},{16,0},{32,16},{48,32},{64,48},{80,64},{96,80},{112,96},{1... | collective-permute-start | bytes 1179656 | tf_op jit(solution)/shard_map/ppermute | solution.py:27
  121.8 4.3 %collective-permute-done.4 = bf16[256,768]{1,0:T(8,128)(2,1)} collective-permute-done((bf16[256,768]{1,0:T(8,128)(2,1)}, bf16[256,768]{1,0:T(8,128)(2,1)}, u32[]{:S(2)}, u32[]{:S(2)}) %collective-permute-start.4) | collective-permute-done | bytes 393248 | tf_op jit(solution)/shard_map/ppermute | solution.py:26
  126.5 40.6 %all-reduce = f32[512]{0:T(512)S(1)} all-reduce(f32[512]{0:T(512)S(1)} %multiply_reduce_fusion), channel_id=4, replica_groups=mesh['ctx'=16,'exp'=16] {'exp'}, use_global_device_ids=true, to_apply=%region_6.7.clone | all-reduce | flops 512 | bytes 4096
  167.2 15.0 %reduce-scatter.2.cloned.1.call-done = bf16[32,4096]{1,0:T(8,128)(2,1)} async-done(((bf16[512,4096]{1,0:T(8,128)(2,1)}), bf16[32,4096]{1,0:T(8,128)(2,1)}) %reduce-scatter.2.cloned.1.call-update) | async-done | bytes 262160 | tf_op jit(solution)/shard_map/reduce_scatter | solution.py:136
  182.2 1.3 multiply_reduce_fusion.1
  183.5 1.5 convolution_convert_fusion.2
  185.0 4.8 %all-to-all-start = ((bf16[16,8,4096]{2,1,0:T(8,128)(2,1)}), bf16[16,8,4096]{2,1,0:T(8,128)(2,1)S(1)}, u32[]{:S(2)}, u32[]{:S(2)}) async-start(bf16[16,8,4096]{2,1,0:T(8,128)(2,1)} %convolution_convert_fusion.2), calls=%async_computation.1 | async-start | bytes 2097152 | tf_op jit(solution)/shard_map/all_to_all | solution.py:167
  190.3 6.9 %collective-permute-done.13 = bf16[256,768]{1,0:T(8,128)(2,1)S(1)} collective-permute-done((bf16[256,768]{1,0:T(8,128)(2,1)}, bf16[256,768]{1,0:T(8,128)(2,1)S(1)}, u32[]{:S(2)}, u32[]{:S(2)}) %collective-permute-start.13) | collective-permute-done | bytes 393248 | tf_op jit(solution)/shard_map/ppermute | solution.py:27
  197.2 2.2 collective-permute-start.14
  199.4 1.8 collective-permute-done.6
  201.2 12.1 %collective-permute-done.14 = bf16[256,768]{1,0:T(8,128)(2,1)} collective-permute-done((bf16[256,768]{1,0:T(8,128)(2,1)S(1)}, bf16[256,768]{1,0:T(8,128)(2,1)}, u32[]{:S(2)}, u32[]{:S(2)}) %collective-permute-start.14) | collective-permute-done | bytes 393248 | tf_op jit(solution)/shard_map/ppermute | solution.py:27
  213.3 2.3 collective-permute-start.15
  215.6 1.5 collective-permute-done.7
  217.3 49.1 %all-gather.7.cloned.1.call-done = bf16[1,4096,1536]{2,1,0:T(8,128)(2,1)} async-done(((bf16[1,256,1536]{2,1,0:T(8,128)(2,1)}), bf16[1,4096,1536]{2,1,0:T(8,128)(2,1)}) %all-gather.7.cloned.1.call-update) | async-done | bytes 12582928 | tf_op jit(solution)/shard_map/all_gather | solution.py:170
  266.5 6.6 %convolution_convert_fusion.1 = bf16[16,128,1536]{2,1,0:T(8,128)(2,1)S(1)} fusion(bf16[16,256,1536]{2,1,0:T(8,128)(2,1)} %bitcast.136, bf16[128,16,256]{2,1,0:T(8,128)(2,1)S(1)} %bitcast.137), kind=kOutput, calls=%fused_computation.5 | convolution fusion | flops 1613758464 | bytes 19922944 | tf_op jit(solution)/shard_map/rkw,kwf->krf/dot_general | solution.py:172
  274.1 1.3 constant_dynamic-update-slice_fusion.31
  275.5 1.3 constant_dynamic-update-slice_fusion.30
  277.1 1.3 constant_dynamic-update-slice_fusion.28
  278.5 1.3 constant_dynamic-update-slice_fusion.27
  279.8 1.3 constant_dynamic-update-slice_fusion.26
  282.6 1.3 constant_dynamic-update-slice_fusion.20
  283.9 1.3 constant_dynamic-update-slice_fusion.19
  285.4 1.3 constant_dynamic-update-slice_fusion.17
  286.7 1.3 constant_dynamic-update-slice_fusion.16
  288.3 1.1 fusion.21
  289.3 7.2 %all-to-all-start.1 = ((bf16[16,8,4096]{2,1,0:T(8,128)(2,1)}), bf16[16,8,4096]{2,1,0:T(8,128)(2,1)S(1)}, u32[]{:S(2)}, u32[]{:S(2)}) async-start(bf16[16,8,4096]{2,1,0:T(8,128)(2,1)} %fusion.21), calls=%async_computation.2 | async-start | bytes 2097152 | tf_op jit(solution)/shard_map/all_to_all | solution.py:189
  297.2 17.6 %all-to-all-done.1 = bf16[16,8,4096]{2,1,0:T(8,128)(2,1)S(1)} async-done(((bf16[16,8,4096]{2,1,0:T(8,128)(2,1)}), bf16[16,8,4096]{2,1,0:T(8,128)(2,1)S(1)}, u32[]{:S(2)}, u32[]{:S(2)}) %all-to-all-start.1) | async-done | bytes 1048608 | tf_op jit(solution)/shard_map/all_to_all | solution.py:189
  314.8 1.5 convolution_bitcast_fusion
  (174 shorter events, 23.3 us)
Async XLA Ops:
  7.2 289.4 %copy-start = (bf16[4096,72]{0,1:T(8,128)(2,1)S(1)}, bf16[4096,72]{0,1:T(8,128)(2,1)}, u32[]{:S(2)}) copy-start(bf16[4096,72]{0,1:T(8,128)(2,1)} %param.31) | copy-start | bytes 1769476
  7.2 62.9 %all-gather.5.cloned.1.call-start = ((), (), s32[]{:S(2)}) async-start(), calls=%async_computation.3 | async-start | bytes 4456448 | tf_op jit(solution)/shard_map/all_gather | solution.py:40
  8.9 10.9 %collective-permute-start = (bf16[3,768]{0,1:T(8,128)(2,1)S(1)}, bf16[3,768]{0,1:T(8,128)(2,1)S(1)}, u32[]{:S(2)}, u32[]{:S(2)}) collective-permute-start(bf16[3,768]{0,1:T(8,128)(2,1)S(1)} %copy.91), channel_id=1, source_target_pairs={{0,16},{16,32},{32,48},{48,64},{64,80},{80,96},{96,112},{112,128},... | collective-permute-start | bytes 13832 | tf_op jit(solution)/shard_map/ppermute | solution.py:35
  20.3 3.1 copy-start.2
  20.3 23.6 %copy-start.4 = (bf16[512,128]{1,0:T(8,128)(2,1)}, bf16[512,128]{1,0:T(8,128)(2,1)S(1)}, u32[]{:S(2)}) copy-start(bf16[512,128]{1,0:T(8,128)(2,1)S(1)} %get-tuple-element.87) | copy-start | bytes 393220
  22.6 2.4 copy-start.7
  22.6 2.6 copy-start.28
  23.4 20.4 %copy-start.3 = (bf16[512,128]{1,0:T(8,128)(2,1)S(1)}, bf16[512,128]{1,0:T(8,128)(2,1)}, u32[]{:S(2)}) copy-start(bf16[512,128]{1,0:T(8,128)(2,1)} %copy-done.2) | copy-start | bytes 393220
  25.0 157.2 %reduce-scatter.2.cloned.1.call-start = ((), (), s32[]{:S(2)}) async-start(), calls=%async_computation.4 | async-start | bytes 4456448 | tf_op jit(solution)/shard_map/reduce_scatter | solution.py:136
  70.2 3.0 copy-start.25
  70.2 3.0 copy-start.26
  76.0 2.2 copy-start.29
  76.0 2.2 copy-start.30
  82.7 16.2 %copy-start.22 = (s32[32,10]{0,1:T(8,128)S(1)}, s32[32,10]{0,1:T(8,128)}, u32[]{:S(2)}) copy-start(s32[32,10]{0,1:T(8,128)} %param.32) | copy-start | bytes 3844
  82.8 16.3 %copy-start.27 = (s32[1,32]{1,0:T(1,128)S(1)}, s32[1,32]{1,0:T(1,128)}, u32[]{:S(2)}) copy-start(s32[1,32]{1,0:T(1,128)} %param.33) | copy-start | bytes 388
  82.8 17.0 %copy-start.32 = (u32[256]{0:T(256)S(1)}, u32[256]{0:T(256)}, u32[]{:S(2)}) copy-start(u32[256]{0:T(256)} %constant.88) | copy-start | bytes 3076
  82.8 100.7 %copy-start.23 = (f32[4096]{0:T(1024)S(1)}, f32[4096]{0:T(1024)}, u32[]{:S(2)}) copy-start(f32[4096]{0:T(1024)} %param.30) | copy-start | bytes 49156
  82.8 183.7 %all-gather.7.cloned.1.call-start = ((), (), s32[]{:S(2)}) async-start(), calls=%async_computation.5 | async-start | bytes 13369344 | tf_op jit(solution)/shard_map/all_gather | solution.py:170
  83.7 7.2 %collective-permute-start.1 = (bf16[256,768]{1,0:T(8,128)(2,1)S(1)}, bf16[256,768]{1,0:T(8,128)(2,1)S(1)}, u32[]{:S(2)}, u32[]{:S(2)}) collective-permute-start(bf16[256,768]{1,0:T(8,128)(2,1)S(1)} %bitcast.149), channel_id=1, source_target_pairs={{0,16},{16,32},{32,48},{48,64},{64,80},{80,96},{96,112},{112,128},... | collective-permute-start | bytes 1179656 | tf_op jit(solution)/shard_map/ppermute | solution.py:26
  85.3 6.5 %collective-permute-start.9 = (bf16[256,768]{1,0:T(8,128)(2,1)S(1)}, bf16[256,768]{1,0:T(8,128)(2,1)S(1)}, u32[]{:S(2)}, u32[]{:S(2)}) collective-permute-start(bf16[256,768]{1,0:T(8,128)(2,1)S(1)} %bitcast.150), channel_id=1, source_target_pairs={{0,240},{16,0},{32,16},{48,32},{64,48},{80,64},{96,80},{112,96},{1... | collective-permute-start | bytes 1179656 | tf_op jit(solution)/shard_map/ppermute | solution.py:27
  90.9 7.2 %collective-permute-start.2 = (bf16[256,768]{1,0:T(8,128)(2,1)S(1)}, bf16[256,768]{1,0:T(8,128)(2,1)S(1)}, u32[]{:S(2)}, u32[]{:S(2)}) collective-permute-start(bf16[256,768]{1,0:T(8,128)(2,1)S(1)} %collective-permute-done.1), channel_id=1, source_target_pairs={{0,16},{16,32},{32,48},{48,64},{64,80},{80,96},{96,112},{112,128},... | collective-permute-start | bytes 1179656 | tf_op jit(solution)/shard_map/ppermute | solution.py:26
  91.8 93.2 %copy-start.10 = (bf16[256,768]{1,0:T(8,128)(2,1)}, bf16[256,768]{1,0:T(8,128)(2,1)S(1)}, u32[]{:S(2)}) copy-start(bf16[256,768]{1,0:T(8,128)(2,1)S(1)} %collective-permute-done.9) | copy-start | bytes 1179652
  91.8 9.2 %collective-permute-start.10 = (bf16[256,768]{1,0:T(8,128)(2,1)S(1)}, bf16[256,768]{1,0:T(8,128)(2,1)S(1)}, u32[]{:S(2)}, u32[]{:S(2)}) collective-permute-start(bf16[256,768]{1,0:T(8,128)(2,1)S(1)} %collective-permute-done.9), channel_id=1, source_target_pairs={{0,240},{16,0},{32,16},{48,32},{64,48},{80,64},{96,80},{112,96},{1... | collective-permute-start | bytes 1179656 | tf_op jit(solution)/shard_map/ppermute | solution.py:27
  98.2 86.8 %copy-start.16 = (bf16[256,768]{1,0:T(8,128)(2,1)}, bf16[256,768]{1,0:T(8,128)(2,1)S(1)}, u32[]{:S(2)}) copy-start(bf16[256,768]{1,0:T(8,128)(2,1)S(1)} %collective-permute-done.2) | copy-start | bytes 1179652
  98.2 18.5 %collective-permute-start.3 = (bf16[256,768]{1,0:T(8,128)(2,1)S(1)}, bf16[256,768]{1,0:T(8,128)(2,1)}, u32[]{:S(2)}, u32[]{:S(2)}) collective-permute-start(bf16[256,768]{1,0:T(8,128)(2,1)S(1)} %collective-permute-done.2), channel_id=1, source_target_pairs={{0,16},{16,32},{32,48},{48,64},{64,80},{80,96},{96,112},{112,128},... | collective-permute-start | bytes 1179656 | tf_op jit(solution)/shard_map/ppermute | solution.py:26
  101.1 83.9 %copy-start.14 = (bf16[256,768]{1,0:T(8,128)(2,1)}, bf16[256,768]{1,0:T(8,128)(2,1)S(1)}, u32[]{:S(2)}) copy-start(bf16[256,768]{1,0:T(8,128)(2,1)S(1)} %collective-permute-done.10) | copy-start | bytes 1179652
  101.1 17.4 %collective-permute-start.11 = (bf16[256,768]{1,0:T(8,128)(2,1)S(1)}, bf16[256,768]{1,0:T(8,128)(2,1)}, u32[]{:S(2)}, u32[]{:S(2)}) collective-permute-start(bf16[256,768]{1,0:T(8,128)(2,1)S(1)} %collective-permute-done.10), channel_id=1, source_target_pairs={{0,240},{16,0},{32,16},{48,32},{64,48},{80,64},{96,80},{112,96},{1... | collective-permute-start | bytes 1179656 | tf_op jit(solution)/shard_map/ppermute | solution.py:27
  116.6 9.5 %collective-permute-start.4 = (bf16[256,768]{1,0:T(8,128)(2,1)}, bf16[256,768]{1,0:T(8,128)(2,1)}, u32[]{:S(2)}, u32[]{:S(2)}) collective-permute-start(bf16[256,768]{1,0:T(8,128)(2,1)} %collective-permute-done.3), channel_id=1, source_target_pairs={{0,16},{16,32},{32,48},{48,64},{64,80},{80,96},{96,112},{112,128},... | collective-permute-start | bytes 1179656 | tf_op jit(solution)/shard_map/ppermute | solution.py:26
  118.5 71.3 %collective-permute-start.12 = (bf16[256,768]{1,0:T(8,128)(2,1)}, bf16[256,768]{1,0:T(8,128)(2,1)}, u32[]{:S(2)}, u32[]{:S(2)}) collective-permute-start(bf16[256,768]{1,0:T(8,128)(2,1)} %collective-permute-done.11), channel_id=1, source_target_pairs={{0,240},{16,0},{32,16},{48,32},{64,48},{80,64},{96,80},{112,96},{1... | collective-permute-start | bytes 1179656 | tf_op jit(solution)/shard_map/ppermute | solution.py:27
  126.1 63.7 %collective-permute-start.5 = (bf16[256,768]{1,0:T(8,128)(2,1)}, bf16[256,768]{1,0:T(8,128)(2,1)}, u32[]{:S(2)}, u32[]{:S(2)}) collective-permute-start(bf16[256,768]{1,0:T(8,128)(2,1)} %collective-permute-done.4), channel_id=1, source_target_pairs={{0,16},{16,32},{32,48},{48,64},{64,80},{80,96},{96,112},{112,128},... | collective-permute-start | bytes 1179656 | tf_op jit(solution)/shard_map/ppermute | solution.py:26
  183.5 113.1 %copy-start.1 = (f32[32,4096]{1,0:T(8,128)}, f32[32,4096]{1,0:T(8,128)S(1)}, u32[]{:S(2)}) copy-start(f32[32,4096]{1,0:T(8,128)S(1)} %get-tuple-element.83) | copy-start | bytes 1572868
  185.0 32.1 %all-to-all-start = ((bf16[16,8,4096]{2,1,0:T(8,128)(2,1)}), bf16[16,8,4096]{2,1,0:T(8,128)(2,1)S(1)}, u32[]{:S(2)}, u32[]{:S(2)}) async-start(bf16[16,8,4096]{2,1,0:T(8,128)(2,1)} %convolution_convert_fusion.2), calls=%async_computation.1 | async-start | bytes 2097152 | tf_op jit(solution)/shard_map/all_to_all | solution.py:167
  189.8 7.4 %collective-permute-start.13 = (bf16[256,768]{1,0:T(8,128)(2,1)}, bf16[256,768]{1,0:T(8,128)(2,1)S(1)}, u32[]{:S(2)}, u32[]{:S(2)}) collective-permute-start(bf16[256,768]{1,0:T(8,128)(2,1)} %collective-permute-done.12), channel_id=1, source_target_pairs={{0,240},{16,0},{32,16},{48,32},{64,48},{80,64},{96,80},{112,96},{1... | collective-permute-start | bytes 1179656 | tf_op jit(solution)/shard_map/ppermute | solution.py:27
  189.9 11.3 %collective-permute-start.6 = (bf16[256,768]{1,0:T(8,128)(2,1)}, bf16[256,768]{1,0:T(8,128)(2,1)S(1)}, u32[]{:S(2)}, u32[]{:S(2)}) collective-permute-start(bf16[256,768]{1,0:T(8,128)(2,1)} %collective-permute-done.5), channel_id=1, source_target_pairs={{0,16},{16,32},{32,48},{48,64},{64,80},{80,96},{96,112},{112,128},... | collective-permute-start | bytes 1179656 | tf_op jit(solution)/shard_map/ppermute | solution.py:26
  197.2 19.8 %copy-start.18 = (bf16[256,768]{1,0:T(8,128)(2,1)}, bf16[256,768]{1,0:T(8,128)(2,1)S(1)}, u32[]{:S(2)}) copy-start(bf16[256,768]{1,0:T(8,128)(2,1)S(1)} %collective-permute-done.13) | copy-start | bytes 1179652
  197.2 16.0 %collective-permute-start.14 = (bf16[256,768]{1,0:T(8,128)(2,1)S(1)}, bf16[256,768]{1,0:T(8,128)(2,1)}, u32[]{:S(2)}, u32[]{:S(2)}) collective-permute-start(bf16[256,768]{1,0:T(8,128)(2,1)S(1)} %collective-permute-done.13), channel_id=1, source_target_pairs={{0,240},{16,0},{32,16},{48,32},{64,48},{80,64},{96,80},{112,96},{1... | collective-permute-start | bytes 1179656 | tf_op jit(solution)/shard_map/ppermute | solution.py:27
  201.2 15.9 %copy-start.20 = (bf16[256,768]{1,0:T(8,128)(2,1)}, bf16[256,768]{1,0:T(8,128)(2,1)S(1)}, u32[]{:S(2)}) copy-start(bf16[256,768]{1,0:T(8,128)(2,1)S(1)} %collective-permute-done.6) | copy-start | bytes 1179652
  201.2 15.9 %collective-permute-start.7 = (bf16[256,768]{1,0:T(8,128)(2,1)S(1)}, bf16[256,768]{1,0:T(8,128)(2,1)}, u32[]{:S(2)}, u32[]{:S(2)}) collective-permute-start(bf16[256,768]{1,0:T(8,128)(2,1)S(1)} %collective-permute-done.6), channel_id=1, source_target_pairs={{0,16},{16,32},{32,48},{48,64},{64,80},{80,96},{96,112},{112,128},... | collective-permute-start | bytes 1179656 | tf_op jit(solution)/shard_map/ppermute | solution.py:26
  213.3 73.5 %collective-permute-start.15 = (bf16[256,768]{1,0:T(8,128)(2,1)}, bf16[256,768]{1,0:T(8,128)(2,1)}, u32[]{:S(2)}, u32[]{:S(2)}) collective-permute-start(bf16[256,768]{1,0:T(8,128)(2,1)} %collective-permute-done.14), channel_id=1, source_target_pairs={{0,240},{16,0},{32,16},{48,32},{64,48},{80,64},{96,80},{112,96},{1... | collective-permute-start | bytes 1179656 | tf_op jit(solution)/shard_map/ppermute | solution.py:27
  217.0 57.1 %collective-permute-start.8 = (bf16[256,768]{1,0:T(8,128)(2,1)}, bf16[256,768]{1,0:T(8,128)(2,1)}, u32[]{:S(2)}, u32[]{:S(2)}) collective-permute-start(bf16[256,768]{1,0:T(8,128)(2,1)} %collective-permute-done.7), channel_id=1, source_target_pairs={{0,16},{16,32},{32,48},{48,64},{64,80},{80,96},{96,112},{112,128},... | collective-permute-start | bytes 1179656 | tf_op jit(solution)/shard_map/ppermute | solution.py:26
  274.0 2.8 copy-start.21
  274.1 7.0 %copy-start.17 = (bf16[256,768]{1,0:T(8,128)(2,1)S(1)}, bf16[256,768]{1,0:T(8,128)(2,1)}, u32[]{:S(2)}) copy-start(bf16[256,768]{1,0:T(8,128)(2,1)} %copy-done.16) | copy-start | bytes 1179652
  275.5 5.9 %copy-start.13 = (bf16[256,768]{1,0:T(8,128)(2,1)S(1)}, bf16[256,768]{1,0:T(8,128)(2,1)}, u32[]{:S(2)}) copy-start(bf16[256,768]{1,0:T(8,128)(2,1)} %copy-done.12) | copy-start | bytes 1179652
  276.8 4.9 %copy-start.9 = (bf16[1,256,768]{2,1,0:T(8,128)(2,1)S(1)}, bf16[1,256,768]{2,1,0:T(8,128)(2,1)}, u32[]{:S(2)}) copy-start(bf16[1,256,768]{2,1,0:T(8,128)(2,1)} %param.35) | copy-start | bytes 1179652
  277.1 4.9 %copy-start.11 = (bf16[256,768]{1,0:T(8,128)(2,1)S(1)}, bf16[256,768]{1,0:T(8,128)(2,1)}, u32[]{:S(2)}) copy-start(bf16[256,768]{1,0:T(8,128)(2,1)} %copy-done.10) | copy-start | bytes 1179652
  278.5 3.8 %copy-start.15 = (bf16[256,768]{1,0:T(8,128)(2,1)S(1)}, bf16[256,768]{1,0:T(8,128)(2,1)}, u32[]{:S(2)}) copy-start(bf16[256,768]{1,0:T(8,128)(2,1)} %copy-done.14) | copy-start | bytes 1179652
  281.4 3.8 %copy-start.19 = (bf16[256,768]{1,0:T(8,128)(2,1)S(1)}, bf16[256,768]{1,0:T(8,128)(2,1)}, u32[]{:S(2)}) copy-start(bf16[256,768]{1,0:T(8,128)(2,1)} %copy-done.18) | copy-start | bytes 1179652
  289.3 25.4 %all-to-all-start.1 = ((bf16[16,8,4096]{2,1,0:T(8,128)(2,1)}), bf16[16,8,4096]{2,1,0:T(8,128)(2,1)S(1)}, u32[]{:S(2)}, u32[]{:S(2)}) async-start(bf16[16,8,4096]{2,1,0:T(8,128)(2,1)} %fusion.21), calls=%async_computation.2 | async-start | bytes 2097152 | tf_op jit(solution)/shard_map/all_to_all | solution.py:189
  (6 other events, 7.0 us)
Sparse Core Ops, SparseCore 0:
  25.1 44.9 all-gather.4
  82.9 99.2 reduce-scatter.1
  184.0 82.3 all-gather.6
